TPU v7x, 32 devices: a whole 2x2x4 slice. The times are simulated.
32 devices in a mesh: gx: 4 (over z), gy: 8 (over y, x, core).
Axes of the slice: x: 2, y: 2, z: 4, core: 2. Of those that a mesh axis runs over, the one named last changes fastest.
Arguments:
- partials: float32 [8192, 512], P(('gx', 'gy')), may hold values from -6 to 6
- partial_ids: int32 [32, 256], replicated, may hold values from 0 to 127
- read_lists: int32 [32, 1024], replicated, may hold values from 0 to 127
- sources: int32 [32, 8192], P(('gx', 'gy')), may hold values from 0 to 1023
- targets: int32 [32, 8192], P(('gx', 'gy')), may hold values from 0 to 127
- kernels: float32 [8, 512, 512], replicated, may hold values from -0.03125 to 0.03125
Outputs:
- local_expansions: float32 [4096, 512], P(('gx', 'gy'))
All inputs are finite; a program needn't handle non-finite values.
Results may differ from a plain program's by a relative error of at most 0.0003.
Values sent between devices are 32-bit elements; how exact they have to be, the bound alone decides.
A program may use at most 192 MiB of HBM per device.

v0:
```python
import jax
import jax.numpy as jnp
from jax import lax
from jax.sharding import PartitionSpec as P

OCT_DEV = 128
DIRS = 8


def body(partials, partial_ids, read_lists, sources, targets, kernels):
    devices = lax.axis_size(("gx", "gy"))
    device = lax.axis_index(("gx", "gy"))
    width = partials.shape[1]
    per_owner = partials.shape[0] // devices
    per_reader = read_lists.shape[1] // devices
    reads_total = devices * per_reader
    octant_iota = jnp.arange(OCT_DEV, dtype=jnp.int32)
    received = lax.all_to_all(partials, ("gx", "gy"), split_axis=0, concat_axis=0, tiled=True)
    column_ids = lax.dynamic_slice_in_dim(partial_ids, device * per_owner, per_owner, 1).reshape(-1)
    selector = (octant_iota[:, None] == column_ids[None, :]).astype(jnp.float32)
    density = jnp.dot(
        selector, received, precision=lax.Precision.HIGHEST, preferred_element_type=jnp.float32
    )
    wanted = lax.dynamic_slice_in_dim(read_lists, device * per_reader, per_reader, 1).reshape(-1)
    pick = (wanted[:, None] == octant_iota[None, :]).astype(jnp.float32)
    outgoing = jnp.dot(
        pick, density, precision=lax.Precision.HIGHEST, preferred_element_type=jnp.float32
    )
    read_rows_local = lax.all_to_all(
        outgoing, ("gx", "gy"), split_axis=0, concat_axis=0, tiled=True
    )
    per_dir = sources.shape[1] // DIRS
    source_blocks = sources[0].reshape(DIRS, per_dir)
    target_blocks = targets[0].reshape(DIRS, per_dir)
    read_iota = jnp.arange(reads_total, dtype=jnp.int32)
    total = jnp.zeros((OCT_DEV, width), jnp.float32)
    for direction in range(DIRS):
        target_pick = (octant_iota[:, None] == target_blocks[direction][None, :]).astype(
            jnp.bfloat16
        )
        source_pick = (source_blocks[direction][:, None] == read_iota[None, :]).astype(jnp.bfloat16)
        counts = jnp.dot(target_pick, source_pick, preferred_element_type=jnp.float32)
        collected = jnp.dot(
            counts,
            read_rows_local,
            precision=lax.Precision.HIGHEST,
            preferred_element_type=jnp.float32,
        )
        total = total + jnp.einsum(
            "op,qp->oq", collected, kernels[direction], precision=lax.Precision.HIGHEST
        )
    return total


def solution(mesh):
    return jax.shard_map(
        body,
        mesh=mesh,
        in_specs=(
            P(("gx", "gy"), None),
            P(),
            P(),
            P(("gx", "gy"), None),
            P(("gx", "gy"), None),
            P(),
        ),
        out_specs=P(("gx", "gy"), None),
        check_vma=False,
    )
```

profile of v0, /device:TPU:0, one launch (start us, length us, event | category | flops | bytes accessed | tf_op | source)
XLA Modules:
  0.0 98.3 jit_solution(4819504336925815839)
XLA Ops:
  0.0 0.0 copy-start
  0.0 7.3 %all-to-all-start = ((f32[32,8,512]{2,1,0:T(8,128)}), f32[32,8,512]{2,1,0:T(8,128)S(1)}, u32[]{:S(2)}, u32[]{:S(2)}) async-start(f32[32,8,512]{2,1,0:T(8,128)} %bitcast.82), calls=%async_computation | async-start | bytes 1048576 | tf_op jit(solution)/shard_map/all_to_all | solution.py:18
  7.4 0.8 constant_dynamic-slice_fusion
  8.2 0.1 eq.283
  8.2 0.0 copy-done
  8.3 0.1 constant_dynamic-slice_fusion.1
  8.3 0.1 eq.278
  8.4 14.6 %all-to-all-done = f32[32,8,512]{2,1,0:T(8,128)S(1)} async-done(((f32[32,8,512]{2,1,0:T(8,128)}), f32[32,8,512]{2,1,0:T(8,128)S(1)}, u32[]{:S(2)}, u32[]{:S(2)}) %all-to-all-start) | async-done | bytes 524320 | tf_op jit(solution)/shard_map/all_to_all | solution.py:18
  23.0 0.3 fusion.33
  23.3 2.4 %fusion.35 = f32[1024,512]{1,0:T(8,128)} fusion(f32[128,512]{1,0:T(8,128)S(1)} %fusion.33, s32[1024]{0:T(1024)S(1)} %eq.278), kind=kOutput, calls=%fused_computation.59 | convolution fusion | flops 805437440 | bytes 2363392 | tf_op jit(solution)/shard_map/dot_general | solution.py:26
  25.7 3.0 %all-to-all-start.1 = ((f32[32,32,512]{2,1,0:T(8,128)}), f32[32,32,512]{2,1,0:T(8,128)S(1)}, u32[]{:S(2)}, u32[]{:S(2)}) async-start(f32[32,32,512]{2,1,0:T(8,128)} %bitcast.81), calls=%async_computation.1 | async-start | bytes 4194304 | tf_op jit(solution)/shard_map/all_to_all | solution.py:29
  28.7 0.0 copy-done.7
  28.7 0.0 copy-done.8
  28.7 1.1 %fusion = f32[128,1024]{1,0:T(8,128)S(1)} fusion(s32[1024]{0:T(1024)S(1)} %bitcast.98, s32[1024]{0:T(1024)S(1)} %bitcast.93), kind=kOutput, calls=%fused_computation.8 | convolution fusion | flops 269615104 | bytes 532480 | tf_op jit(solution)/shard_map/dot_general | solution.py:42
  29.8 1.1 %fusion.1 = f32[128,1024]{1,0:T(8,128)S(1)} fusion(s32[1024]{0:T(1024)S(1)} %bitcast.97, s32[1024]{0:T(1024)S(1)} %bitcast.91), kind=kOutput, calls=%fused_computation.9 | convolution fusion | flops 269615104 | bytes 532480 | tf_op jit(solution)/shard_map/dot_general | solution.py:42
  30.8 1.9 %fusion.2 = f32[128,1024]{1,0:T(8,128)} fusion(s32[1024]{0:T(1024)S(1)} %bitcast.96, s32[1024]{0:T(1024)S(1)} %bitcast.89), kind=kOutput, calls=%fused_computation.10 | convolution fusion | flops 269615104 | bytes 532480 | tf_op jit(solution)/shard_map/dot_general | solution.py:42
  32.7 1.9 %fusion.3 = f32[128,1024]{1,0:T(8,128)} fusion(s32[1024]{0:T(1024)S(1)} %bitcast.95, s32[1024]{0:T(1024)S(1)} %bitcast.88), kind=kOutput, calls=%fused_computation.11 | convolution fusion | flops 269615104 | bytes 532480 | tf_op jit(solution)/shard_map/dot_general | solution.py:42
  34.5 1.9 %fusion.4 = f32[128,1024]{1,0:T(8,128)} fusion(s32[1024]{0:T(1024)S(1)} %bitcast.94, s32[1024]{0:T(1024)S(1)} %bitcast.86), kind=kOutput, calls=%fused_computation.12 | convolution fusion | flops 269615104 | bytes 532480 | tf_op jit(solution)/shard_map/dot_general | solution.py:42
  36.4 1.9 %fusion.5 = f32[128,1024]{1,0:T(8,128)} fusion(s32[1024]{0:T(1024)S(1)} %bitcast.92, s32[1024]{0:T(1024)S(1)} %bitcast.85), kind=kOutput, calls=%fused_computation.13 | convolution fusion | flops 269615104 | bytes 532480 | tf_op jit(solution)/shard_map/dot_general | solution.py:42
  38.2 1.9 %fusion.6 = f32[128,1024]{1,0:T(8,128)} fusion(s32[1024]{0:T(1024)S(1)} %bitcast.90, s32[1024]{0:T(1024)S(1)} %bitcast.84), kind=kOutput, calls=%fused_computation.14 | convolution fusion | flops 269615104 | bytes 532480 | tf_op jit(solution)/shard_map/dot_general | solution.py:42
  40.1 1.9 %fusion.7 = f32[128,1024]{1,0:T(8,128)} fusion(s32[1024]{0:T(1024)S(1)} %bitcast.87, s32[1024]{0:T(1024)S(1)} %bitcast.83), kind=kOutput, calls=%fused_computation.15 | convolution fusion | flops 269615104 | bytes 532480 | tf_op jit(solution)/shard_map/dot_general | solution.py:42
  42.0 35.4 %all-to-all-done.1 = f32[32,32,512]{2,1,0:T(8,128)S(1)} async-done(((f32[32,32,512]{2,1,0:T(8,128)}), f32[32,32,512]{2,1,0:T(8,128)S(1)}, u32[]{:S(2)}, u32[]{:S(2)}) %all-to-all-start.1) | async-done | bytes 2097184 | tf_op jit(solution)/shard_map/all_to_all | solution.py:29
  77.4 1.3 %fusion.48 = f32[128,512]{1,0:T(8,128)S(1)} fusion(f32[128,1024]{1,0:T(8,128)S(1)} %fusion, f32[1024,512]{1,0:T(8,128)S(1)} %bitcast.71), kind=kOutput, calls=%fused_computation.75 | convolution fusion | flops 805306368 | bytes 2883584 | tf_op jit(solution)/shard_map/dot_general | solution.py:43
  78.7 0.0 copy-start.3
  78.7 1.3 %fusion.49 = f32[128,512]{1,0:T(8,128)S(1)} fusion(f32[128,1024]{1,0:T(8,128)S(1)} %fusion.1, f32[1024,512]{1,0:T(8,128)S(1)} %bitcast.72), kind=kOutput, calls=%fused_computation.76 | convolution fusion | flops 805306368 | bytes 2883584 | tf_op jit(solution)/shard_map/dot_general | solution.py:43
  80.0 0.0 copy-done.1
  80.0 0.0 copy-start.4
  80.0 0.0 slice-start
  80.0 1.3 %fusion.50 = f32[128,512]{1,0:T(8,128)S(1)} fusion(f32[128,1024]{1,0:T(8,128)S(1)} %copy-done.1, f32[1024,512]{1,0:T(8,128)S(1)} %bitcast.73), kind=kOutput, calls=%fused_computation.77 | convolution fusion | flops 805306368 | bytes 2883584 | tf_op jit(solution)/shard_map/dot_general | solution.py:43
  81.3 0.0 copy-done.2
  81.3 0.0 copy-start.5
  81.3 1.5 %fusion.51 = f32[128,512]{1,0:T(8,128)S(1)} fusion(f32[128,1024]{1,0:T(8,128)S(1)} %copy-done.2, f32[1024,512]{1,0:T(8,128)S(1)} %bitcast.74), kind=kOutput, calls=%fused_computation.78 | convolution fusion | flops 805306368 | bytes 2883584 | tf_op jit(solution)/shard_map/dot_general | solution.py:43
  82.8 0.0 copy-done.3
  82.9 0.0 copy-start.6
  82.9 1.3 %fusion.52 = f32[128,512]{1,0:T(8,128)S(1)} fusion(f32[128,1024]{1,0:T(8,128)S(1)} %copy-done.3, f32[1024,512]{1,0:T(8,128)S(1)} %bitcast.75), kind=kOutput, calls=%fused_computation.79 | convolution fusion | flops 805306368 | bytes 2883584 | tf_op jit(solution)/shard_map/dot_general | solution.py:43
  84.2 0.0 slice-start.1
  84.2 1.3 %fusion.53 = f32[128,512]{1,0:T(8,128)S(1)} fusion(f32[128,1024]{1,0:T(8,128)S(1)} %copy-done.4, f32[1024,512]{1,0:T(8,128)S(1)} %bitcast.76), kind=kOutput, calls=%fused_computation.80 | convolution fusion | flops 805306368 | bytes 2883584 | tf_op jit(solution)/shard_map/dot_general | solution.py:43
  85.5 1.3 %fusion.54 = f32[128,512]{1,0:T(8,128)S(1)} fusion(f32[128,1024]{1,0:T(8,128)S(1)} %copy-done.5, f32[1024,512]{1,0:T(8,128)S(1)} %bitcast.77), kind=kOutput, calls=%fused_computation.81 | convolution fusion | flops 805306368 | bytes 2883584 | tf_op jit(solution)/shard_map/dot_general | solution.py:43
  86.8 0.0 copy-done.6
  86.8 1.3 %fusion.55 = f32[128,512]{1,0:T(8,128)S(1)} fusion(f32[128,1024]{1,0:T(8,128)S(1)} %copy-done.6, f32[1024,512]{1,0:T(8,128)S(1)} %bitcast.78), kind=kOutput, calls=%fused_computation.82 | convolution fusion | flops 805306368 | bytes 2883584 | tf_op jit(solution)/shard_map/dot_general | solution.py:43
  88.1 1.2 %fusion.23 = f32[128,512]{1,0:T(8,128)S(1)} fusion(f32[128,512]{1,0:T(8,128)S(1)} %fusion.48, f32[8,512,512]{2,1,0:T(8,128)S(1)} %bitcast.80), kind=kOutput, calls=%fused_computation.38 | convolution fusion | flops 402653184 | bytes 1572864 | tf_op jit(solution)/shard_map/op,qp->oq/dot_general | solution.py:49
  89.3 1.2 %convolution_add_fusion.6 = f32[128,512]{1,0:T(8,128)S(1)} fusion(f32[128,512]{1,0:T(8,128)S(1)} %fusion.23, f32[128,512]{1,0:T(8,128)S(1)} %fusion.49, f32[8,512,512]{2,1,0:T(8,128)S(1)} %bitcast.80), kind=kOutput, calls=%fused_computation.30 | convolution fusion | flops 402718720 | bytes 1835008 | tf_op jit(solution)/shard_map/op,qp->oq/dot_general | solution.py:49
  90.5 1.2 %convolution_add_fusion.5 = f32[128,512]{1,0:T(8,128)S(1)} fusion(f32[128,512]{1,0:T(8,128)S(1)} %convolution_add_fusion.6, f32[128,512]{1,0:T(8,128)S(1)} %fusion.50, f32[8,512,512]{2,1,0:T(8,128)S(1)} %bitcast.80), kind=kOutput, calls=%fused_computation.29 | convolution fusion | flops 402718720 | bytes 1835008 | tf_op jit(solution)/shard_map/op,qp->oq/dot_general | solution.py:49
  91.7 1.2 %convolution_add_fusion.4 = f32[128,512]{1,0:T(8,128)S(1)} fusion(f32[128,512]{1,0:T(8,128)S(1)} %convolution_add_fusion.5, f32[128,512]{1,0:T(8,128)S(1)} %fusion.51, f32[8,512,512]{2,1,0:T(8,128)S(1)} %bitcast.80), kind=kOutput, calls=%fused_computation.28 | convolution fusion | flops 402718720 | bytes 1835008 | tf_op jit(solution)/shard_map/op,qp->oq/dot_general | solution.py:49
  92.9 1.2 %convolution_add_fusion.3 = f32[128,512]{1,0:T(8,128)S(1)} fusion(f32[128,512]{1,0:T(8,128)S(1)} %convolution_add_fusion.4, f32[128,512]{1,0:T(8,128)S(1)} %fusion.52, f32[8,512,512]{2,1,0:T(8,128)S(1)} %bitcast.80), kind=kOutput, calls=%fused_computation.27 | convolution fusion | flops 402718720 | bytes 1835008 | tf_op jit(solution)/shard_map/op,qp->oq/dot_general | solution.py:49
  94.0 1.2 %convolution_add_fusion.2 = f32[128,512]{1,0:T(8,128)S(1)} fusion(f32[128,512]{1,0:T(8,128)S(1)} %convolution_add_fusion.3, f32[128,512]{1,0:T(8,128)S(1)} %fusion.53, f32[8,512,512]{2,1,0:T(8,128)S(1)} %bitcast.80), kind=kOutput, calls=%fused_computation.26 | convolution fusion | flops 402718720 | bytes 1835008 | tf_op jit(solution)/shard_map/op,qp->oq/dot_general | solution.py:49
  95.2 1.2 %convolution_add_fusion.1 = f32[128,512]{1,0:T(8,128)S(1)} fusion(f32[128,512]{1,0:T(8,128)S(1)} %convolution_add_fusion.2, f32[128,512]{1,0:T(8,128)S(1)} %fusion.54, f32[8,512,512]{2,1,0:T(8,128)S(1)} %bitcast.80), kind=kOutput, calls=%fused_computation.25 | convolution fusion | flops 402718720 | bytes 1835008 | tf_op jit(solution)/shard_map/op,qp->oq/dot_general | solution.py:49
  96.4 1.9 %convolution_add_fusion = f32[128,512]{1,0:T(8,128)} fusion(f32[128,512]{1,0:T(8,128)S(1)} %convolution_add_fusion.1, f32[128,512]{1,0:T(8,128)S(1)} %fusion.55, f32[8,512,512]{2,1,0:T(8,128)S(1)} %bitcast.80), kind=kOutput, calls=%fused_computation.24 | convolution fusion | flops 402718720 | bytes 1835008 | tf_op jit(solution)/shard_map/op,qp->oq/dot_general | solution.py:49
  (11 shorter events, 0.0 us)
Async XLA Ops:
  0.0 8.2 %copy-start = (s32[32,1024]{1,0:T(8,128)S(1)}, s32[32,1024]{1,0:T(8,128)}, u32[]{:S(2)}) copy-start(s32[32,1024]{1,0:T(8,128)} %param.8) | copy-start | bytes 393220
  0.0 28.6 %copy-start.7 = (s32[1,8192]{1,0:T(1,128)S(1)}, s32[1,8192]{1,0:T(1,128)}, u32[]{:S(2)}) copy-start(s32[1,8192]{1,0:T(1,128)} %param.10) | copy-start | bytes 98308
  0.0 28.7 %copy-start.8 = (s32[1,8192]{1,0:T(1,128)S(1)}, s32[1,8192]{1,0:T(1,128)}, u32[]{:S(2)}) copy-start(s32[1,8192]{1,0:T(1,128)} %param.9) | copy-start | bytes 98308
  0.0 23.0 %all-to-all-start = ((f32[32,8,512]{2,1,0:T(8,128)}), f32[32,8,512]{2,1,0:T(8,128)S(1)}, u32[]{:S(2)}, u32[]{:S(2)}) async-start(f32[32,8,512]{2,1,0:T(8,128)} %bitcast.82), calls=%async_computation | async-start | bytes 1048576 | tf_op jit(solution)/shard_map/all_to_all | solution.py:18
  25.7 51.7 %all-to-all-start.1 = ((f32[32,32,512]{2,1,0:T(8,128)}), f32[32,32,512]{2,1,0:T(8,128)S(1)}, u32[]{:S(2)}, u32[]{:S(2)}) async-start(f32[32,32,512]{2,1,0:T(8,128)} %bitcast.81), calls=%async_computation.1 | async-start | bytes 4194304 | tf_op jit(solution)/shard_map/all_to_all | solution.py:29
  77.4 2.6 %copy-start.1 = (f32[128,1024]{1,0:T(8,128)S(1)}, f32[128,1024]{1,0:T(8,128)}, u32[]{:S(2)}) copy-start(f32[128,1024]{1,0:T(8,128)} %fusion.2) | copy-start | bytes 1572868
  77.4 3.9 %copy-start.2 = (f32[128,1024]{1,0:T(8,128)S(1)}, f32[128,1024]{1,0:T(8,128)}, u32[]{:S(2)}) copy-start(f32[128,1024]{1,0:T(8,128)} %fusion.3) | copy-start | bytes 1572868
  78.7 4.2 %copy-start.3 = (f32[128,1024]{1,0:T(8,128)S(1)}, f32[128,1024]{1,0:T(8,128)}, u32[]{:S(2)}) copy-start(f32[128,1024]{1,0:T(8,128)} %fusion.4) | copy-start | bytes 1572868
  80.0 4.2 %copy-start.4 = (f32[128,1024]{1,0:T(8,128)S(1)}, f32[128,1024]{1,0:T(8,128)}, u32[]{:S(2)}) copy-start(f32[128,1024]{1,0:T(8,128)} %fusion.5) | copy-start | bytes 1572868
  80.0 8.1 %slice-start = ((s8[8388608]{0:T(1024)(128)(4,1)}), s8[4194304]{0:T(1024)(128)(4,1)S(1)}, s32[]{:S(2)}) async-start(s8[8388608]{0:T(1024)(128)(4,1)} %bitcast.79), calls=%async_computation.2 | async-start | bytes 8388608
  81.3 4.2 %copy-start.5 = (f32[128,1024]{1,0:T(8,128)S(1)}, f32[128,1024]{1,0:T(8,128)}, u32[]{:S(2)}) copy-start(f32[128,1024]{1,0:T(8,128)} %fusion.6) | copy-start | bytes 1572868
  82.9 3.9 %copy-start.6 = (f32[128,1024]{1,0:T(8,128)S(1)}, f32[128,1024]{1,0:T(8,128)}, u32[]{:S(2)}) copy-start(f32[128,1024]{1,0:T(8,128)} %fusion.7) | copy-start | bytes 1572868
  84.2 3.9 %slice-start.1 = ((s8[8388608]{0:T(1024)(128)(4,1)}), s8[4194304]{0:T(1024)(128)(4,1)S(1)}, s32[]{:S(2)}) async-start(s8[8388608]{0:T(1024)(128)(4,1)} %bitcast.79), calls=%async_computation.3 | async-start | bytes 8388608
where the time goes:
time: 98.6 us; the launch traced here: 98.3 us
  waiting for transfers between devices  50 us (51%)
  matrix products  36.6 us (37%)
  starting transfers between devices  10.3 us (10%)
  local copies, waits for them, and re-layouts  1.1 us (1%)
    all_to_all x1, waiting for transfers between devices, body(): lax.all_to_all(outgoing, ('gx', 'gy'), split_axis=0, concat_axis=0, tiled...  35.4 us
    all_to_all x1, waiting for transfers between devices, body(): lax.all_to_all(partials, ('gx', 'gy'), split_axis=0, concat_axis=0, tiled...  14.6 us
    dot_general x8, matrix products, body(): jnp.dot(target_pick, source_pick, preferred_element_type=jnp.float32)  13.2 us
    dot_general x8, matrix products, body(): jnp.dot(counts, read_rows_local, precision=lax.Precision.HIGHEST, preferr...  10.5 us
    dot_general x8, matrix products, body(): jnp.einsum('op,qp->oq', collected, kernels[direction], precision=lax.Prec...  10.1 us
    all_to_all x1, starting transfers between devices, body(): lax.all_to_all(partials, ('gx', 'gy'), split_axis=0, concat_axis=0, tiled...  7.33 us
    all_to_all x1, starting transfers between devices, body(): lax.all_to_all(outgoing, ('gx', 'gy'), split_axis=0, concat_axis=0, tiled...  2.97 us
    dot_general x1, matrix products, body(): jnp.dot(pick, density, precision=lax.Precision.HIGHEST, preferred_element...  2.37 us
  transfers between devices with their start and end apart: 2, of which 2 were waited for; matrix products, arithmetic and copies ran while one was open for 15% of the time, Pallas kernels for 0%

commit v1 on v0

v1 whole, which is shorter than its diff:
```python
import functools

import jax
import jax.numpy as jnp
from jax import lax
from jax.experimental import pallas as pl
from jax.experimental.pallas import tpu as pltpu
from jax.sharding import PartitionSpec as P

OCT_DEV = 128
DIRS = 8
MESH = pl.DeviceIdType.MESH
F32 = jnp.float32
BF16 = jnp.bfloat16


def split2(x):
    hi = x.astype(BF16)
    return hi, (x - hi.astype(F32)).astype(BF16)


def onehot(mask):
    return jnp.where(mask, 1.0, 0.0).astype(F32).astype(BF16)


def dot(a, b):
    return lax.dot_general(a, b, (((1,), (0,)), ((), ())), preferred_element_type=F32)


def dot_nt(a, b):
    return lax.dot_general(a, b, (((1,), (1,)), ((), ())), preferred_element_type=F32)


def kernel(
    gxn, gyn, per_owner, per_reader,
    partials, pids, rlists, src, tgt, kern, out,
    recv, dens, outgoing, rows, chi, clo, acc, khi, klo, kbuf, wcol,
    s1, r1, l1, ksem, ag_send, ag_recv, pl_send, pl_recv,
):
    n = gxn * gyn
    gx = lax.axis_index("gx")
    gy = lax.axis_index("gy")
    me = gx * gyn + gy
    slots = n * per_owner
    half = gyn * per_reader
    per_dir = src.shape[1] // DIRS

    barrier = pltpu.get_barrier_semaphore()

    def peer(step):
        o = lax.rem(me + step, n)
        return o, (o // gyn, lax.rem(o, gyn))

    def greet(step, c):
        _, dev = peer(step)
        pl.semaphore_signal(barrier, inc=1, device_id=dev, device_id_type=MESH)
        return c

    lax.fori_loop(1, n, greet, 0)

    def kcopy(d):
        s = lax.rem(d, 2)
        return pltpu.make_async_copy(kern.at[d], kbuf.at[s], ksem.at[s])

    own = pltpu.make_async_copy(
        partials.at[pl.ds(pl.multiple_of(me * per_owner, 8), per_owner)],
        recv.at[pl.ds(pl.multiple_of(me * per_owner, 8), per_owner)],
        l1,
    )
    own.start()
    kcopy(0).start()
    kcopy(1).start()
    pl.semaphore_wait(barrier, n - 1)

    def send1(step, c):
        o, dev = peer(step)
        pltpu.make_async_remote_copy(
            src_ref=partials.at[pl.ds(pl.multiple_of(o * per_owner, 8), per_owner)],
            dst_ref=recv.at[pl.ds(pl.multiple_of(me * per_owner, 8), per_owner)],
            send_sem=s1, recv_sem=r1, device_id=dev, device_id_type=MESH,
        ).start()
        return c

    lax.fori_loop(1, n, send1, 0)

    def counts(d, c):
        at = pl.ds(pl.multiple_of(d * per_dir, 128), per_dir)
        s = src[:, at]
        t = tgt[:, at]
        h = jnp.zeros_like(s)
        for k in range(1, gxn):
            h = h + jnp.where(s >= k * half, 1, 0)
        lo = s - h * half
        comb = h * OCT_DEV + t
        tpick = onehot(lax.broadcasted_iota(jnp.int32, (gxn * OCT_DEV, per_dir), 0) == comb)
        spick = onehot(lax.broadcasted_iota(jnp.int32, (half, per_dir), 0) == lo)
        cnt = dot_nt(tpick, spick)
        hi, low = split2(cnt)
        row = pl.ds(pl.multiple_of(d * OCT_DEV, OCT_DEV), OCT_DEV)
        for k in range(gxn):
            chi[k, row, :] = hi[k * OCT_DEV:(k + 1) * OCT_DEV]
            clo[k, row, :] = low[k * OCT_DEV:(k + 1) * OCT_DEV]
        kcopy(d).wait()
        kh, kl = split2(kbuf[lax.rem(d, 2)])
        khi[d] = kh
        klo[d] = kl

        @pl.when(d + 2 < DIRS)
        def _():
            kcopy(d + 2).start()

        return c

    lax.fori_loop(0, DIRS, counts, 0)

    plane = rlists[pl.ds(pl.multiple_of(gx * gyn, 8), gyn), :].astype(F32).astype(BF16)
    c_iota = lax.broadcasted_iota(jnp.int32, (half, 1), 0)
    q_of = lax.rem(c_iota, per_reader)
    j_of = lax.div(c_iota, per_reader)
    j_mask = lax.broadcasted_iota(jnp.int32, (half, gyn), 1) == j_of
    s_iota = lax.broadcasted_iota(jnp.int32, (half, plane.shape[1]), 1)

    def picks(z, c):
        sel = onehot(s_iota == (z * gyn + gy) * per_reader + q_of)
        m = dot_nt(sel, plane)
        col = jnp.sum(jnp.where(j_mask, m, 0.0), axis=1, keepdims=True)
        wcol[z] = onehot(
            lax.broadcasted_iota(jnp.int32, (half, OCT_DEV), 1) == col.astype(jnp.int32)
        )
        return c

    lax.fori_loop(0, gxn, picks, 0)

    e_iota = lax.broadcasted_iota(jnp.int32, (1, slots), 1)
    sel = onehot(
        lax.broadcasted_iota(jnp.int32, (slots, slots), 0)
        == me * per_owner + lax.rem(e_iota, per_owner)
    )
    m = dot(pids[...].astype(F32).astype(BF16), sel)
    keep = lax.broadcasted_iota(jnp.int32, (n, slots), 0) == lax.div(e_iota, per_owner)
    ids = jnp.sum(jnp.where(keep, m, 0.0), axis=0, keepdims=True).astype(jnp.int32)
    selector = onehot(lax.broadcasted_iota(jnp.int32, (OCT_DEV, slots), 0) == ids)
    acc[...] = jnp.zeros_like(acc)

    own.wait()
    rest = recv.at[pl.ds(0, (n - 1) * per_owner)]
    all1 = pltpu.make_async_remote_copy(
        src_ref=rest, dst_ref=rest, send_sem=s1, recv_sem=r1,
        device_id=(gx, gy), device_id_type=MESH,
    )
    all1.wait_recv()
    p_hi, p_lo = split2(recv[...])
    dens[gx] = dot(selector, p_hi) + dot(selector, p_lo)

    def along(z, up):
        to = gx + 1 if up else gx - 1
        return pltpu.make_async_remote_copy(
            src_ref=dens.at[z], dst_ref=dens.at[z],
            send_sem=ag_send.at[1 if up else 0, z], recv_sem=ag_recv.at[z],
            device_id=(to, gy), device_id_type=MESH,
        )

    def spread(z):
        d_hi, d_lo = split2(dens[z])
        outgoing[z] = dot(wcol[z], d_hi) + dot(wcol[z], d_lo)
        base = pl.multiple_of(z * half + gy * per_reader, 8)

        def one(step, c):
            j = lax.rem(gy + step, gyn)
            pltpu.make_async_remote_copy(
                src_ref=outgoing.at[z, pl.ds(pl.multiple_of(j * per_reader, 8), per_reader)],
                dst_ref=rows.at[pl.ds(base, per_reader)],
                send_sem=pl_send.at[z], recv_sem=pl_recv.at[z],
                device_id=(gx, j), device_id_type=MESH,
            ).start()
            return c

        lax.fori_loop(1, gyn, one, 0)
        rows[pl.ds(base, per_reader), :] = outgoing[
            z, pl.ds(pl.multiple_of(gy * per_reader, 8), per_reader), :
        ]

    def plane_all(z):
        part = rows.at[pl.ds(0, (gyn - 1) * per_reader)]
        return pltpu.make_async_remote_copy(
            src_ref=part, dst_ref=part, send_sem=pl_send.at[z], recv_sem=pl_recv.at[z],
            device_id=(gx, gy), device_id_type=MESH,
        )

    def collect(z):
        plane_all(z).wait_recv()
        r_hi, r_lo = split2(rows[pl.ds(pl.multiple_of(z * half, 8), half), :])
        acc[...] += dot(chi[z], r_hi) + dot(chi[z], r_lo) + dot(clo[z], r_hi)

    @pl.when(gx + 1 < gxn)
    def _():
        along(gx, True).start()

    @pl.when(gx > 0)
    def _():
        along(gx, False).start()

    spread(gx)

    def place(j):
        k = j // 2 + 1
        return gx + jnp.where(lax.rem(j, 2) == 0, -k, k)

    def phase2(j, c):
        z = place(j)
        ok = (z >= 0) & (z < gxn)

        @pl.when(ok)
        def _():
            along(z, True).wait_recv()

        @pl.when(ok & (z < gx) & (gx + 1 < gxn))
        def _():
            along(z, True).start()

        @pl.when(ok & (z > gx) & (gx > 0))
        def _():
            along(z, False).start()

        @pl.when(ok)
        def _():
            spread(z)

        y = jnp.where(j == 0, gx, place(jnp.maximum(j - 1, 0)))

        @pl.when((y >= 0) & (y < gxn))
        def _():
            collect(y)

        return c

    steps = 2 * (gxn - 1)
    lax.fori_loop(0, steps, phase2, 0)
    last = place(steps - 1)

    @pl.when((last >= 0) & (last < gxn))
    def _():
        collect(last)

    out[...] = jnp.zeros_like(out)

    def final(d, c):
        c_hi, c_lo = split2(acc[pl.ds(pl.multiple_of(d * OCT_DEV, OCT_DEV), OCT_DEV), :])
        out[...] += dot_nt(c_hi, khi[d]) + dot_nt(c_lo, khi[d]) + dot_nt(c_hi, klo[d])
        return c

    lax.fori_loop(0, DIRS, final, 0)

    all1.wait_send()

    def drain(z, c):
        plane_all(z).wait_send()

        @pl.when((z <= gx) & (gx + 1 < gxn))
        def _():
            along(z, True).wait_send()

        @pl.when((z >= gx) & (gx > 0))
        def _():
            along(z, False).wait_send()

        return c

    lax.fori_loop(0, gxn, drain, 0)


def body(partials, partial_ids, read_lists, sources, targets, kernels):
    gxn = lax.axis_size("gx")
    gyn = lax.axis_size("gy")
    n = gxn * gyn
    width = partials.shape[1]
    per_owner = partials.shape[0] // n
    reads = read_lists.shape[1]
    per_reader = reads // n
    half = gyn * per_reader
    vmem = pl.BlockSpec(memory_space=pltpu.VMEM)
    hbm = pl.BlockSpec(memory_space=pl.ANY)
    dma = pltpu.SemaphoreType.DMA
    return pl.pallas_call(
        functools.partial(kernel, gxn, gyn, per_owner, per_reader),
        out_shape=jax.ShapeDtypeStruct((OCT_DEV, width), F32),
        in_specs=[hbm, vmem, vmem, vmem, vmem, hbm],
        out_specs=vmem,
        scratch_shapes=[
            pltpu.VMEM((n * per_owner, width), F32),
            pltpu.VMEM((gxn, OCT_DEV, width), F32),
            pltpu.VMEM((gxn, half, width), F32),
            pltpu.VMEM((reads, width), F32),
            pltpu.VMEM((gxn, DIRS * OCT_DEV, half), BF16),
            pltpu.VMEM((gxn, DIRS * OCT_DEV, half), BF16),
            pltpu.VMEM((DIRS * OCT_DEV, width), F32),
            pltpu.VMEM((DIRS, width, width), BF16),
            pltpu.VMEM((DIRS, width, width), BF16),
            pltpu.VMEM((2, width, width), F32),
            pltpu.VMEM((gxn, half, OCT_DEV), BF16),
            dma, dma, dma, dma((2,)), dma((2, gxn)), dma((gxn,)), dma((gxn,)), dma((gxn,)),
        ],
        compiler_params=pltpu.CompilerParams(
            collective_id=0, has_side_effects=True, vmem_limit_bytes=62 * 1024 * 1024
        ),
    )(partials, partial_ids, read_lists, sources, targets, kernels)


def solution(mesh):
    return jax.shard_map(
        body,
        mesh=mesh,
        in_specs=(
            P(("gx", "gy"), None),
            P(),
            P(),
            P(("gx", "gy"), None),
            P(("gx", "gy"), None),
            P(),
        ),
        out_specs=P(("gx", "gy"), None),
        check_vma=False,
    )
```

time: 98.6 us -> 65.1 us (0.66)
  Pallas kernels: 0 us -> 62.8 us
  waiting for transfers between devices: 50 us -> 0 us
  matrix products: 36.6 us -> 0 us
  starting transfers between devices: 10.3 us -> 0 us
    pallas_call x0 -> x1, Pallas kernels: none -> 62.8 us  [body(): pl.pallas_call(functools.partial(kernel, gxn, gyn, per_owner, per_reader)...]
    all_to_all x2 -> x0, waiting for transfers between devices: 50 us -> none  [the longest x1 35.4 us: body(): lax.all_to_all(outgoing, ('gx', 'gy'), split_axis=0, concat_axis=0, tiled...]
    dot_general x26 -> x0, matrix products: 36.6 us -> none  [the longest x8 13.2 us: body(): jnp.dot(target_pick, source_pick, preferred_element_type=jnp.float32)]
    all_to_all x2 -> x0, starting transfers between devices: 10.3 us -> none  [the longest x1 7.33 us: body(): lax.all_to_all(partials, ('gx', 'gy'), split_axis=0, concat_axis=0, tiled...]
    unnamed x22 -> x1, local copies, waits for them, and re-layouts: 0.05 us -> 1.67 us
  transfers between devices with their start and end apart: 2 -> 0, of which waited for: 2 -> 0; matrix products, arithmetic and copies ran while one was open for 15% -> 0% of each run, Pallas kernels for 0% -> 0%
where the time goes in v1:
time: 65.1 us; the launch traced here: 64.4 us
  Pallas kernels  62.8 us (96%)
  local copies, waits for them, and re-layouts  1.67 us (3%)
    pallas_call x1, Pallas kernels, body(): pl.pallas_call(functools.partial(kernel, gxn, gyn, per_owner, per_reader)...  62.8 us
    unnamed x1, local copies, waits for them, and re-layouts  1.67 us

profile of v1, /device:TPU:0, one launch (start us, length us, event | category | flops | bytes accessed | tf_op | source)
XLA Modules:
  0.0 64.4 jit_solution(2973476159563387623)
XLA Ops:
  0.0 62.8 %shard_map.64 = f32[128,512]{1,0:T(8,128)} custom-call(f32[256,512]{1,0:T(8,128)} %partials.1, s32[32,256]{1,0:T(8,128)} %pids.1, s32[32,1024]{1,0:T(8,128)} %rlists.1, s32[1,8192]{1,0:T(1,128)} %src.1, s32[1,8192]{1,0:T(1,128)} %tgt.1, f32[8,512,512]{2,1,0:T(8,128)} %kern.1), custom_call_target="tpu_custom_call" | custom-call | tf_op jit(solution)/shard_map/pallas_call | solution.py:284
  62.8 1.7 %copy.8 = f32[128,512]{1,0:T(8,128)} copy(f32[128,512]{1,0:T(8,128)} %shard_map.64) | data formatting | bytes 524288

commit v2 on v1

--- a/solution.py
+++ b/solution.py
@@ -29,6 +29,15 @@
 
 def dot_nt(a, b):
     return lax.dot_general(a, b, (((1,), (1,)), ((), ())), preferred_element_type=F32)
+
+
+def partner(i, k):
+    bit = 1
+    while bit <= k:
+        if k & bit:
+            i = i + bit - 2 * bit * lax.rem(i // bit, 2)
+        bit *= 2
+    return i
 
 
 def kernel(
@@ -45,6 +54,7 @@
     half = gyn * per_reader
     per_dir = src.shape[1] // DIRS
 
+    order = sorted(range(1, gyn), key=lambda k: (bin(k >> 1).count("1") or gyn, k & 1, k))
     barrier = pltpu.get_barrier_semaphore()
 
     def peer(step):
@@ -165,17 +175,14 @@
         outgoing[z] = dot(wcol[z], d_hi) + dot(wcol[z], d_lo)
         base = pl.multiple_of(z * half + gy * per_reader, 8)
 
-        def one(step, c):
-            j = lax.rem(gy + step, gyn)
+        for k in order:
+            j = partner(gy, k)
             pltpu.make_async_remote_copy(
                 src_ref=outgoing.at[z, pl.ds(pl.multiple_of(j * per_reader, 8), per_reader)],
                 dst_ref=rows.at[pl.ds(base, per_reader)],
                 send_sem=pl_send.at[z], recv_sem=pl_recv.at[z],
                 device_id=(gx, j), device_id_type=MESH,
             ).start()
-            return c
-
-        lax.fori_loop(1, gyn, one, 0)
         rows[pl.ds(base, per_reader), :] = outgoing[
             z, pl.ds(pl.multiple_of(gy * per_reader, 8), per_reader), :
         ]
@@ -190,7 +197,11 @@
     def collect(z):
         plane_all(z).wait_recv()
         r_hi, r_lo = split2(rows[pl.ds(pl.multiple_of(z * half, 8), half), :])
-        acc[...] += dot(chi[z], r_hi) + dot(chi[z], r_lo) + dot(clo[z], r_hi)
+        c_hi = chi[z]
+        acc[...] += dot(
+            jnp.concatenate([c_hi, c_hi, clo[z]], axis=1),
+            jnp.concatenate([r_hi, r_lo, r_hi], axis=0),
+        )
 
     @pl.when(gx + 1 < gxn)
     def _():
@@ -202,51 +213,70 @@
 
     spread(gx)
 
-    def place(j):
-        k = j // 2 + 1
-        return gx + jnp.where(lax.rem(j, 2) == 0, -k, k)
-
-    def phase2(j, c):
-        z = place(j)
-        ok = (z >= 0) & (z < gxn)
-
-        @pl.when(ok)
-        def _():
-            along(z, True).wait_recv()
-
-        @pl.when(ok & (z < gx) & (gx + 1 < gxn))
-        def _():
-            along(z, True).start()
-
-        @pl.when(ok & (z > gx) & (gx > 0))
-        def _():
-            along(z, False).start()
-
-        @pl.when(ok)
-        def _():
-            spread(z)
-
-        y = jnp.where(j == 0, gx, place(jnp.maximum(j - 1, 0)))
-
-        @pl.when((y >= 0) & (y < gxn))
-        def _():
-            collect(y)
-
-        return c
-
-    steps = 2 * (gxn - 1)
-    lax.fori_loop(0, steps, phase2, 0)
-    last = place(steps - 1)
-
-    @pl.when((last >= 0) & (last < gxn))
-    def _():
-        collect(last)
-
+    def inside(z):
+        return (z >= 0) & (z < gxn)
+
+    def level(k, c):
+        low = gx - k
+        high = gx + k
+
+        @pl.when(inside(low))
+        def _():
+            along(low, True).wait_recv()
+
+        @pl.when(inside(low) & (gx + 1 < gxn))
+        def _():
+            along(low, True).start()
+
+        @pl.when(inside(high))
+        def _():
+            along(high, False).wait_recv()
+
+        @pl.when(inside(high) & (gx > 0))
+        def _():
+            along(high, False).start()
+
+        def side(i, c):
+            z = gx + (2 * i - 1) * k
+
+            @pl.when(inside(z))
+            def _():
+                spread(z)
+
+            return c
+
+        lax.fori_loop(0, 2, side, 0)
+
+        def back(i, c):
+            z = gx + (2 * i - 1) * (k - 1)
+
+            @pl.when(inside(z) & ((k > 1) | (i == 0)))
+            def _():
+                collect(z)
+
+            return c
+
+        lax.fori_loop(0, 2, back, 0)
+        return c
+
+    lax.fori_loop(1, gxn, level, 0)
+
+    def rest_of(i, c):
+        z = gx + (2 * i - 1) * (gxn - 1)
+
+        @pl.when(inside(z))
+        def _():
+            collect(z)
+
+        return c
+
+    lax.fori_loop(0, 2, rest_of, 0)
     out[...] = jnp.zeros_like(out)
 
     def final(d, c):
         c_hi, c_lo = split2(acc[pl.ds(pl.multiple_of(d * OCT_DEV, OCT_DEV), OCT_DEV), :])
-        out[...] += dot_nt(c_hi, khi[d]) + dot_nt(c_lo, khi[d]) + dot_nt(c_hi, klo[d])
+        both = dot_nt(jnp.concatenate([c_hi, c_lo], axis=0), khi[d])
+        out[...] += both[:OCT_DEV] + both[OCT_DEV:] + dot_nt(c_hi, klo[d])
         return c
 
     lax.fori_loop(0, DIRS, final, 0)

time: 65.1 us -> 56.6 us (0.87)
  Pallas kernels: 62.8 us -> 54.7 us
    pallas_call x1, Pallas kernels: 62.8 us -> 54.7 us  [body(): pl.pallas_call(functools.partial(kernel, gxn, gyn, per_owner, per_reader)...]
where the time goes in v2:
time: 56.6 us; the launch traced here: 56.3 us
  Pallas kernels  54.7 us (97%)
  local copies, waits for them, and re-layouts  1.67 us (3%)
    pallas_call x1, Pallas kernels, body(): pl.pallas_call(functools.partial(kernel, gxn, gyn, per_owner, per_reader)...  54.7 us
    unnamed x1, local copies, waits for them, and re-layouts  1.67 us

profile of v2, /device:TPU:0, one launch (start us, length us, event | category | flops | bytes accessed | tf_op | source)
XLA Modules:
  0.0 56.3 jit_solution(7064616144256514647)
XLA Ops:
  0.0 54.7 %shard_map.64 = f32[128,512]{1,0:T(8,128)} custom-call(f32[256,512]{1,0:T(8,128)} %partials.1, s32[32,256]{1,0:T(8,128)} %pids.1, s32[32,1024]{1,0:T(8,128)} %rlists.1, s32[1,8192]{1,0:T(1,128)} %src.1, s32[1,8192]{1,0:T(1,128)} %tgt.1, f32[8,512,512]{2,1,0:T(8,128)} %kern.1), custom_call_target="tpu_custom_call" | custom-call | tf_op jit(solution)/shard_map/pallas_call | solution.py:314
  54.7 1.7 %copy.8 = f32[128,512]{1,0:T(8,128)} copy(f32[128,512]{1,0:T(8,128)} %shard_map.64) | data formatting | bytes 524288

commit v3 on v2

--- a/solution.py
+++ b/solution.py
@@ -42,9 +42,9 @@
 
 def kernel(
     gxn, gyn, per_owner, per_reader,
-    partials, pids, rlists, src, tgt, kern, out,
-    recv, dens, outgoing, rows, chi, clo, acc, khi, klo, kbuf, wcol,
-    s1, r1, l1, ksem, ag_send, ag_recv, pl_send, pl_recv,
+    partials, pids_hbm, rlists_hbm, src_hbm, tgt_hbm, kern, out,
+    recv, dens, outgoing, rows, chi, clo, acc, khi, klo, kbuf, wcol, pids, rlists, src, tgt,
+    s1, r1, l1, isem, ksem, ag_send, ag_recv, pl_send, pl_recv,
 ):
     n = gxn * gyn
     gx = lax.axis_index("gx")
@@ -53,9 +53,16 @@
     slots = n * per_owner
     half = gyn * per_reader
     per_dir = src.shape[1] // DIRS
+    width = partials.shape[1] // 2
 
     order = sorted(range(1, gyn), key=lambda k: (bin(k >> 1).count("1") or gyn, k & 1, k))
     barrier = pltpu.get_barrier_semaphore()
+    loads = [
+        pltpu.make_async_copy(a, b, isem.at[i])
+        for i, (a, b) in enumerate(
+            ((src_hbm, src), (tgt_hbm, tgt), (rlists_hbm, rlists), (pids_hbm, pids))
+        )
+    ]
 
     def peer(step):
         o = lax.rem(me + step, n)
@@ -78,6 +85,8 @@
         l1,
     )
     own.start()
+    for load in loads:
+        load.start()
     kcopy(0).start()
     kcopy(1).start()
     pl.semaphore_wait(barrier, n - 1)
@@ -92,6 +101,9 @@
         return c
 
     lax.fori_loop(1, n, send1, 0)
+
+    for load in loads:
+        load.wait()
 
     def counts(d, c):
         at = pl.ds(pl.multiple_of(d * per_dir, 128), per_dir)
@@ -160,139 +172,149 @@
     )
     all1.wait_recv()
     p_hi, p_lo = split2(recv[...])
-    dens[gx] = dot(selector, p_hi) + dot(selector, p_lo)
-
-    def along(z, up):
+
+    def along(z, up, f):
         to = gx + 1 if up else gx - 1
         return pltpu.make_async_remote_copy(
-            src_ref=dens.at[z], dst_ref=dens.at[z],
-            send_sem=ag_send.at[1 if up else 0, z], recv_sem=ag_recv.at[z],
+            src_ref=dens.at[z, f], dst_ref=dens.at[z, f],
+            send_sem=ag_send.at[1 if up else 0, f, z], recv_sem=ag_recv.at[f, z],
             device_id=(to, gy), device_id_type=MESH,
         )
 
-    def spread(z):
-        d_hi, d_lo = split2(dens[z])
-        outgoing[z] = dot(wcol[z], d_hi) + dot(wcol[z], d_lo)
+    def spread(z, f):
+        d_hi, d_lo = split2(dens[z, f])
+        outgoing[z, f] = dot(wcol[z], d_hi) + dot(wcol[z], d_lo)
         base = pl.multiple_of(z * half + gy * per_reader, 8)
-
         for k in order:
             j = partner(gy, k)
             pltpu.make_async_remote_copy(
-                src_ref=outgoing.at[z, pl.ds(pl.multiple_of(j * per_reader, 8), per_reader)],
-                dst_ref=rows.at[pl.ds(base, per_reader)],
-                send_sem=pl_send.at[z], recv_sem=pl_recv.at[z],
+                src_ref=outgoing.at[z, f, pl.ds(pl.multiple_of(j * per_reader, 8), per_reader)],
+                dst_ref=rows.at[f, pl.ds(base, per_reader)],
+                send_sem=pl_send.at[f, z], recv_sem=pl_recv.at[f, z],
                 device_id=(gx, j), device_id_type=MESH,
             ).start()
-        rows[pl.ds(base, per_reader), :] = outgoing[
-            z, pl.ds(pl.multiple_of(gy * per_reader, 8), per_reader), :
+        rows[f, pl.ds(base, per_reader), :] = outgoing[
+            z, f, pl.ds(pl.multiple_of(gy * per_reader, 8), per_reader), :
         ]
 
-    def plane_all(z):
-        part = rows.at[pl.ds(0, (gyn - 1) * per_reader)]
+    def plane_all(z, f):
+        part = rows.at[f, pl.ds(0, (gyn - 1) * per_reader)]
         return pltpu.make_async_remote_copy(
-            src_ref=part, dst_ref=part, send_sem=pl_send.at[z], recv_sem=pl_recv.at[z],
+            src_ref=part, dst_ref=part, send_sem=pl_send.at[f, z], recv_sem=pl_recv.at[f, z],
             device_id=(gx, gy), device_id_type=MESH,
         )
 
-    def collect(z):
-        plane_all(z).wait_recv()
-        r_hi, r_lo = split2(rows[pl.ds(pl.multiple_of(z * half, 8), half), :])
+    def collect(z, f):
+        plane_all(z, f).wait_recv()
+        r_hi, r_lo = split2(rows[f, pl.ds(pl.multiple_of(z * half, 8), half), :])
         c_hi = chi[z]
-        acc[...] += dot(
+        acc[f] += dot(
             jnp.concatenate([c_hi, c_hi, clo[z]], axis=1),
             jnp.concatenate([r_hi, r_lo, r_hi], axis=0),
         )
 
-    @pl.when(gx + 1 < gxn)
-    def _():
-        along(gx, True).start()
-
-    @pl.when(gx > 0)
-    def _():
-        along(gx, False).start()
-
-    spread(gx)
+    for f in range(2):
+        at = slice(f * width, (f + 1) * width)
+        dens[gx, f] = dot(selector, p_hi[:, at]) + dot(selector, p_lo[:, at])
+
+        @pl.when(gx + 1 < gxn)
+        def _():
+            along(gx, True, f).start()
+
+        @pl.when(gx > 0)
+        def _():
+            along(gx, False, f).start()
+
+        spread(gx, f)
 
     def inside(z):
         return (z >= 0) & (z < gxn)
+
+    last = jnp.where(2 * gx < gxn, gxn - 1, 0)
+
+    def back(k):
+        def one(i, c):
+            z = gx + (2 * i - 1) * k
+
+            @pl.when(inside(z) & (z != last) & ((k > 0) | (i == 0)))
+            def _():
+                for f in range(2):
+                    collect(z, f)
+
+            return c
+
+        lax.fori_loop(0, 2, one, 0)
 
     def level(k, c):
         low = gx - k
         high = gx + k
 
-        @pl.when(inside(low))
+        def part(f, c):
+            @pl.when(inside(low))
+            def _():
+                along(low, True, f).wait_recv()
+
+            @pl.when(inside(low) & (gx + 1 < gxn))
+            def _():
+                along(low, True, f).start()
+
+            @pl.when(inside(high))
+            def _():
+                along(high, False, f).wait_recv()
+
+            @pl.when(inside(high) & (gx > 0))
+            def _():
+                along(high, False, f).start()
+
+            def side(i, c):
+                z = gx + (2 * i - 1) * k
+
+                @pl.when(inside(z))
+                def _():
+                    spread(z, f)
+
+                return c
+
+            lax.fori_loop(0, 2, side, 0)
+            return c
+
+        lax.fori_loop(0, 2, part, 0)
+
+        @pl.when(k > 1)
         def _():
-            along(low, True).wait_recv()
-
-        @pl.when(inside(low) & (gx + 1 < gxn))
-        def _():
-            along(low, True).start()
-
-        @pl.when(inside(high))
-        def _():
-            along(high, False).wait_recv()
-
-        @pl.when(inside(high) & (gx > 0))
-        def _():
-            along(high, False).start()
-
-        def side(i, c):
-            z = gx + (2 * i - 1) * k
-
-            @pl.when(inside(z))
-            def _():
-                spread(z)
-
+            back(k - 2)
+
+        return c
+
+    lax.fori_loop(1, gxn, level, 0)
+    back(gxn - 2)
+    out[...] = jnp.zeros_like(out)
+
+    for f in range(2):
+        collect(last, f)
+        at = slice(f * width, (f + 1) * width)
+
+        def final(d, c):
+            c_hi, c_lo = split2(acc[f, pl.ds(pl.multiple_of(d * OCT_DEV, OCT_DEV), OCT_DEV), :])
+            both = dot_nt(jnp.concatenate([c_hi, c_lo], axis=0), khi[d, :, at])
+            out[...] += both[:OCT_DEV] + both[OCT_DEV:] + dot_nt(c_hi, klo[d, :, at])
             return c
 
-        lax.fori_loop(0, 2, side, 0)
-
-        def back(i, c):
-            z = gx + (2 * i - 1) * (k - 1)
-
-            @pl.when(inside(z) & ((k > 1) | (i == 0)))
-            def _():
-                collect(z)
-
-            return c
-
-        lax.fori_loop(0, 2, back, 0)
-        return c
-
-    lax.fori_loop(1, gxn, level, 0)
-
-    def rest_of(i, c):
-        z = gx + (2 * i - 1) * (gxn - 1)
-
-        @pl.when(inside(z))
-        def _():
-            collect(z)
-
-        return c
-
-    lax.fori_loop(0, 2, rest_of, 0)
-    out[...] = jnp.zeros_like(out)
-
-    def final(d, c):
-        c_hi, c_lo = split2(acc[pl.ds(pl.multiple_of(d * OCT_DEV, OCT_DEV), OCT_DEV), :])
-        both = dot_nt(jnp.concatenate([c_hi, c_lo], axis=0), khi[d])
-        out[...] += both[:OCT_DEV] + both[OCT_DEV:] + dot_nt(c_hi, klo[d])
-        return c
-
-    lax.fori_loop(0, DIRS, final, 0)
+        lax.fori_loop(0, DIRS, final, 0)
 
     all1.wait_send()
 
     def drain(z, c):
-        plane_all(z).wait_send()
-
-        @pl.when((z <= gx) & (gx + 1 < gxn))
-        def _():
-            along(z, True).wait_send()
-
-        @pl.when((z >= gx) & (gx > 0))
-        def _():
-            along(z, False).wait_send()
+        for f in range(2):
+            plane_all(z, f).wait_send()
+
+            @pl.when((z <= gx) & (gx + 1 < gxn))
+            def _():
+                along(z, True, f).wait_send()
+
+            @pl.when((z >= gx) & (gx > 0))
+            def _():
+                along(z, False, f).wait_send()
 
         return c
 
@@ -314,21 +336,26 @@
     return pl.pallas_call(
         functools.partial(kernel, gxn, gyn, per_owner, per_reader),
         out_shape=jax.ShapeDtypeStruct((OCT_DEV, width), F32),
-        in_specs=[hbm, vmem, vmem, vmem, vmem, hbm],
+        in_specs=[hbm] * 6,
         out_specs=vmem,
         scratch_shapes=[
             pltpu.VMEM((n * per_owner, width), F32),
-            pltpu.VMEM((gxn, OCT_DEV, width), F32),
-            pltpu.VMEM((gxn, half, width), F32),
-            pltpu.VMEM((reads, width), F32),
+            pltpu.VMEM((gxn, 2, OCT_DEV, width // 2), F32),
+            pltpu.VMEM((gxn, 2, half, width // 2), F32),
+            pltpu.VMEM((2, reads, width // 2), F32),
             pltpu.VMEM((gxn, DIRS * OCT_DEV, half), BF16),
             pltpu.VMEM((gxn, DIRS * OCT_DEV, half), BF16),
-            pltpu.VMEM((DIRS * OCT_DEV, width), F32),
+            pltpu.VMEM((2, DIRS * OCT_DEV, width // 2), F32),
             pltpu.VMEM((DIRS, width, width), BF16),
             pltpu.VMEM((DIRS, width, width), BF16),
             pltpu.VMEM((2, width, width), F32),
             pltpu.VMEM((gxn, half, OCT_DEV), BF16),
-            dma, dma, dma, dma((2,)), dma((2, gxn)), dma((gxn,)), dma((gxn,)), dma((gxn,)),
+            pltpu.VMEM(partial_ids.shape, jnp.int32),
+            pltpu.VMEM(read_lists.shape, jnp.int32),
+            pltpu.VMEM(sources.shape, jnp.int32),
+            pltpu.VMEM(targets.shape, jnp.int32),
+            dma, dma, dma, dma((4,)), dma((2,)),
+            dma((2, 2, gxn)), dma((2, gxn)), dma((2, gxn)), dma((2, gxn)),
         ],
         compiler_params=pltpu.CompilerParams(
             collective_id=0, has_side_effects=True, vmem_limit_bytes=62 * 1024 * 1024

time: 56.6 us -> 50.8 us (0.90)
  Pallas kernels: 54.7 us -> 48.9 us
    pallas_call x1, Pallas kernels: 54.7 us -> 48.9 us  [body(): pl.pallas_call(functools.partial(kernel, gxn, gyn, per_owner, per_reader)...]
where the time goes in v3:
time: 50.8 us; the launch traced here: 50.6 us
  Pallas kernels  48.9 us (96%)
  local copies, waits for them, and re-layouts  1.67 us (3%)
    pallas_call x1, Pallas kernels, body(): pl.pallas_call(functools.partial(kernel, gxn, gyn, per_owner, per_reader)...  48.9 us
    unnamed x1, local copies, waits for them, and re-layouts  1.67 us

profile of v3, /device:TPU:0, one launch (start us, length us, event | category | flops | bytes accessed | tf_op | source)
XLA Modules:
  0.0 50.6 jit_solution(9185296453517776744)
XLA Ops:
  0.0 48.9 %shard_map.64 = f32[128,512]{1,0:T(8,128)} custom-call(f32[256,512]{1,0:T(8,128)} %partials.1, s32[32,256]{1,0:T(8,128)} %pids_hbm.1, s32[32,1024]{1,0:T(8,128)} %rlists_hbm.1, s32[1,8192]{1,0:T(1,128)} %src_hbm.1, s32[1,8192]{1,0:T(1,128)} %tgt_hbm.1, f32[8,512,512]{2,1,0:T(8,128)} %kern.1), custom_call_target="tpu_custom_call" | custom-call | tf_op jit(solution)/shard_map/pallas_call | solution.py:336
  48.9 1.7 %copy.8 = f32[128,512]{1,0:T(8,128)} copy(f32[128,512]{1,0:T(8,128)} %shard_map.64) | data formatting | bytes 524288

commit v4 on v3

--- a/solution.py
+++ b/solution.py
@@ -300,7 +300,7 @@
             out[...] += both[:OCT_DEV] + both[OCT_DEV:] + dot_nt(c_hi, klo[d, :, at])
             return c
 
-        lax.fori_loop(0, DIRS, final, 0)
+        lax.fori_loop(0, DIRS, final, 0, unroll=4)
 
     all1.wait_send()
 

time: 50.8 us -> 49.6 us (0.976)
  Pallas kernels: 48.9 us -> 47.7 us
    pallas_call x1, Pallas kernels: 48.9 us -> 47.7 us  [body(): pl.pallas_call(functools.partial(kernel, gxn, gyn, per_owner, per_reader)...]
where the time goes in v4:
time: 49.6 us; the launch traced here: 49.4 us
  Pallas kernels  47.7 us (96%)
  local copies, waits for them, and re-layouts  1.67 us (3%)
    pallas_call x1, Pallas kernels, body(): pl.pallas_call(functools.partial(kernel, gxn, gyn, per_owner, per_reader)...  47.7 us
    unnamed x1, local copies, waits for them, and re-layouts  1.67 us

profile of v4, /device:TPU:0, one launch (start us, length us, event | category | flops | bytes accessed | tf_op | source)
XLA Modules:
  0.0 49.4 jit_solution(13761917707461121186)
XLA Ops:
  0.0 47.7 %shard_map.64 = f32[128,512]{1,0:T(8,128)} custom-call(f32[256,512]{1,0:T(8,128)} %partials.1, s32[32,256]{1,0:T(8,128)} %pids_hbm.1, s32[32,1024]{1,0:T(8,128)} %rlists_hbm.1, s32[1,8192]{1,0:T(1,128)} %src_hbm.1, s32[1,8192]{1,0:T(1,128)} %tgt_hbm.1, f32[8,512,512]{2,1,0:T(8,128)} %kern.1), custom_call_target="tpu_custom_call" | custom-call | tf_op jit(solution)/shard_map/pallas_call | solution.py:336
  47.7 1.7 %copy.8 = f32[128,512]{1,0:T(8,128)} copy(f32[128,512]{1,0:T(8,128)} %shard_map.64) | data formatting | bytes 524288
